TPU v7x, 32 devices: a whole 2x2x4 slice. The times are simulated.
32 devices in a mesh: dp: 8 (over z, x), seq: 4 (over y, core).
Axes of the slice: x: 2, y: 2, z: 4, core: 2. Of those that a mesh axis runs over, the one named last changes fastest.
Arguments:
- queries: bfloat16 [8, 512, 2048], P('dp', 'seq'), may hold values from -72 to 72
- hit_keys: bfloat16 [8, 512, 2048], P('dp', 'seq'), may hold values from -12 to 12
- hit_values: bfloat16 [8, 512, 2048], P('dp', 'seq'), may hold values from -6 to 6
- hit_counts: int32 [8], P('dp'), may hold values from 128 to 512, as said below
- master_weight: float32 [8, 256, 2048], P('dp', None, 'seq'), may hold values from -0.5 to 0.5
- first_moment: float32 [8, 256, 2048], P('dp', None, 'seq'), may hold values from -4 to 4
- second_moment: float32 [8, 256, 2048], P('dp', None, 'seq'), may hold values from 0.1 to 4
- gradient: float32 [8, 256, 2048], P('dp', None, 'seq'), may hold values from -6 to 6
- owner_bucket: int32 [8], replicated, may hold values from 0 to 7, each once
Outputs:
- projected: bfloat16 [8, 512, 2048], P('dp', 'seq')
- new_master: float32 [8, 256, 2048], P('dp', None, 'seq')
- new_first: float32 [8, 256, 2048], P('dp', None, 'seq')
- new_second: float32 [8, 256, 2048], P('dp', None, 'seq')
Inputs may be any that keep to these rules, and one draw needn't show every extreme that they name: The valid hits of event e are its first hit_counts[e] slots; some event is full. `owner_bucket`: each bucket is held by exactly one owner.
All inputs are finite; a program needn't handle non-finite values.
Results may differ from a plain program's by a relative error of at most 0.0063.
Values may be sent and summed in bfloat16 or wider, within the bound.
No kernel may reach another device: no remote copies, remote signals or barrier semaphores. Data moves between devices by JAX's collectives and lax.ppermute only.
A program may use at most 64 MiB of HBM per device.

v0:
```python
import jax
import jax.numpy as jnp
from jax import lax
from jax.sharding import PartitionSpec as P

HEAD_DIM = 128
beta_one = 0.9
beta_two = 0.999
learn_rate = 0.003
weight_decay = 0.1
epsilon = 1e-08
step_count = 10.0
block_rows = 512


def adam_update(master_weight, first_moment, second_moment, gradient):
    new_first = beta_one * first_moment + (1.0 - beta_one) * gradient
    new_second = beta_two * second_moment + (1.0 - beta_two) * gradient * gradient
    first_hat = new_first / (1.0 - beta_one**step_count)
    second_hat = new_second / (1.0 - beta_two**step_count)
    new_master = master_weight - learn_rate * (
        first_hat / (jnp.sqrt(second_hat) + epsilon) + weight_decay * master_weight
    )
    return (new_master, new_first, new_second)


def attend_head(head_query, head_keys, head_values, count):
    length = head_query.shape[0]
    block = min(block_rows, length)
    scale = head_query.shape[1] ** (-0.5)
    valid = lax.broadcasted_iota(jnp.int32, (1, length), 1) < count

    def one_block(rows):
        scores = (
            lax.dot_general(
                rows, head_keys, (((1,), (1,)), ((), ())), preferred_element_type=jnp.float32
            )
            * scale
        )
        scores = jnp.where(valid, scores, -jnp.inf)
        top = jnp.max(scores, axis=1, keepdims=True)
        expo = jnp.exp(scores - top)
        weights = (expo / jnp.sum(expo, axis=1, keepdims=True)).astype(jnp.bfloat16)
        return jnp.dot(weights, head_values, preferred_element_type=jnp.float32).astype(
            jnp.bfloat16
        )

    blocks = head_query.reshape(length // block, block, head_query.shape[1])
    return lax.map(one_block, blocks).reshape(length, head_query.shape[1])


def body(
    queries,
    hit_keys,
    hit_values,
    hit_counts,
    master_weight,
    first_moment,
    second_moment,
    gradient,
    owner_bucket,
):
    new_master, new_first, new_second = adam_update(
        master_weight, first_moment, second_moment, gradient
    )
    weight_half = new_master.astype(jnp.bfloat16)
    groups = lax.axis_size("seq")
    owners = lax.axis_size("dp")
    tok_rows = queries.shape[1]
    width = queries.shape[2]
    per_group = width // groups
    heads_here = per_group // HEAD_DIM
    count = hit_counts[0]
    matches = owner_bucket[:, None] == jnp.arange(owners, dtype=jnp.int32)[None, :]
    inverse = jnp.sum(jnp.where(matches, jnp.arange(owners, dtype=jnp.int32)[:, None], 0), axis=0)

    def split_heads(array):
        return array.reshape(1, tok_rows, groups, heads_here, HEAD_DIM)

    query_part = lax.all_to_all(
        split_heads(queries), "seq", split_axis=2, concat_axis=1, tiled=True
    )
    keys_part = lax.all_to_all(
        split_heads(hit_keys), "seq", split_axis=2, concat_axis=1, tiled=True
    )
    values_part = lax.all_to_all(
        split_heads(hit_values), "seq", split_axis=2, concat_axis=1, tiled=True
    )
    n_heads = query_part.shape[3]

    def one_head(index):
        head_query = lax.dynamic_index_in_dim(query_part, index, 3, keepdims=False)[0, :, 0, :]
        head_keys = lax.dynamic_index_in_dim(keys_part, index, 3, keepdims=False)[0, :, 0, :]
        head_values = lax.dynamic_index_in_dim(values_part, index, 3, keepdims=False)[0, :, 0, :]
        return attend_head(head_query, head_keys, head_values, count)

    outputs = lax.map(one_head, jnp.arange(n_heads, dtype=jnp.int32))
    attended = jnp.moveaxis(outputs, 0, 1)[None, :, None, :, :]
    returned = lax.all_to_all(attended, "seq", split_axis=1, concat_axis=2, tiled=True)
    rows_in = returned.reshape(tok_rows, width)
    owned = lax.all_gather(weight_half, "dp", axis=0, tiled=True)
    full = lax.all_gather(owned, "seq", axis=2, tiled=True)
    projection = jnp.take(full, inverse, axis=0).reshape(width, width)
    total = jnp.dot(rows_in, projection, preferred_element_type=jnp.float32)
    projected = total.astype(jnp.bfloat16)[None]
    return (projected, new_master, new_first, new_second)


def solution(mesh):
    return jax.shard_map(
        body,
        mesh=mesh,
        in_specs=(
            P("dp", "seq", None),
            P("dp", "seq", None),
            P("dp", "seq", None),
            P("dp"),
            P("dp", None, "seq"),
            P("dp", None, "seq"),
            P("dp", None, "seq"),
            P("dp", None, "seq"),
            P(),
        ),
        out_specs=(
            P("dp", "seq", None),
            P("dp", None, "seq"),
            P("dp", None, "seq"),
            P("dp", None, "seq"),
        ),
        check_vma=False,
    )
```

profile of v0, /device:TPU:0, one launch (start us, length us, event | category | flops | bytes accessed | tf_op | source)
XLA Modules:
  0.0 175.6 jit_solution(9775890406966182870)
XLA Ops:
  7.2 3.1 %fusion.15 = (bf16[1,256,512]{2,1,0:T(8,128)(2,1)}, f32[1,256,512]{2,1,0:T(8,128)}, f32[1,256,512]{2,1,0:T(8,128)}, f32[1,256,512]{2,1,0:T(8,128)}) fusion(f32[1,256,512]{2,1,0:T(8,128)} %param.15, f32[1,256,512]{2,1,0:T(8,128)} %param.18, f32[1,256,512]{2,1,0:T(8,128)} %param.16, f32[1,256,512]{2,1,0:T(8,128)} %param.17), kind=kLoop, calls=%fused_computation.33 | loop fusion | flops 2097152 | bytes 3932160 | tf_op jit(solution)/shard_map/convert_element_type | solution.py:66
  10.4 52.3 %all-gather.3.cloned.1.call-done = bf16[8,256,512]{2,1,0:T(8,128)(2,1)} async-done(((bf16[1,256,512]{2,1,0:T(8,128)(2,1)}), bf16[8,256,512]{2,1,0:T(8,128)(2,1)}) %all-gather.3.cloned.1.call-update) | async-done | bytes 2097168 | tf_op jit(solution)/shard_map/all_gather | solution.py:101
  62.8 1.3 copy.41
  64.1 1.0 copy.42
  65.1 3.5 %all-to-all-start.1 = ((bf16[1,128,4,4,128]{4,1,3,0,2:T(8,128)(2,1)}), bf16[1,128,4,4,128]{4,1,3,0,2:T(8,128)(2,1)S(1)}, u32[]{:S(2)}, u32[]{:S(2)}) async-start(bf16[1,128,4,4,128]{4,1,3,0,2:T(8,128)(2,1)} %copy.42), calls=%async_computation.1 | async-start | bytes 1048576 | tf_op jit(solution)/shard_map/all_to_all | solution.py:83
  68.9 1.0 copy.45
  69.9 10.8 %all-to-all-done.1 = bf16[1,128,4,4,128]{4,1,3,0,2:T(8,128)(2,1)S(1)} async-done(((bf16[1,128,4,4,128]{4,1,3,0,2:T(8,128)(2,1)}), bf16[1,128,4,4,128]{4,1,3,0,2:T(8,128)(2,1)S(1)}, u32[]{:S(2)}, u32[]{:S(2)}) %all-to-all-start.1) | async-done | bytes 524320 | tf_op jit(solution)/shard_map/all_to_all | solution.py:83
  80.7 3.5 %all-to-all-start.2 = ((bf16[1,128,4,4,128]{4,1,3,0,2:T(8,128)(2,1)}), bf16[1,128,4,4,128]{4,1,3,0,2:T(8,128)(2,1)S(1)}, u32[]{:S(2)}, u32[]{:S(2)}) async-start(bf16[1,128,4,4,128]{4,1,3,0,2:T(8,128)(2,1)} %copy.45), calls=%async_computation.2 | async-start | bytes 1048576 | tf_op jit(solution)/shard_map/all_to_all | solution.py:86
  84.5 1.0 copy.39
  85.5 13.4 %all-to-all-done.2 = bf16[1,128,4,4,128]{4,1,3,0,2:T(8,128)(2,1)S(1)} async-done(((bf16[1,128,4,4,128]{4,1,3,0,2:T(8,128)(2,1)}), bf16[1,128,4,4,128]{4,1,3,0,2:T(8,128)(2,1)S(1)}, u32[]{:S(2)}, u32[]{:S(2)}) %all-to-all-start.2) | async-done | bytes 524320 | tf_op jit(solution)/shard_map/all_to_all | solution.py:86
  99.0 3.5 %all-to-all-start = ((bf16[1,128,4,4,128]{4,1,3,0,2:T(8,128)(2,1)}), bf16[1,128,4,4,128]{4,1,3,0,2:T(8,128)(2,1)S(1)}, u32[]{:S(2)}, u32[]{:S(2)}) async-start(bf16[1,128,4,4,128]{4,1,3,0,2:T(8,128)(2,1)} %copy.39), calls=%async_computation | async-start | bytes 1048576 | tf_op jit(solution)/shard_map/all_to_all | solution.py:80
  102.6 14.5 %all-to-all-done = bf16[1,128,4,4,128]{4,1,3,0,2:T(8,128)(2,1)S(1)} async-done(((bf16[1,128,4,4,128]{4,1,3,0,2:T(8,128)(2,1)}), bf16[1,128,4,4,128]{4,1,3,0,2:T(8,128)(2,1)S(1)}, u32[]{:S(2)}, u32[]{:S(2)}) %all-to-all-start) | async-done | bytes 524320 | tf_op jit(solution)/shard_map/all_to_all | solution.py:80
  117.2 16.6 %while.10 = (s32[]{:T(128)}, bf16[4,512,128]{2,1,0:T(8,128)(2,1)S(1)}, s32[]{:T(128)}, s32[4]{0:T(128)S(1)}, bf16[1,512,1,4,128]{4,1,3,2,0:T(8,128)(2,1)S(1)}, /...) while((s32[]{:T(128)}, ...), condition=%wide.region_3.4_spmd, body=%wide.region_0.3_spmd.sunk | while | flops 136379904 | bytes 3682463 | solution.py:97
  117.3 0.6 dynamic_slice.40
  119.8 0.7 iota_compare_fusion.3
  121.0 0.4 fusion.27
  121.4 0.6 dynamic_slice.40
  123.9 0.7 iota_compare_fusion.3
  125.1 0.4 fusion.27
  125.6 0.6 dynamic_slice.40
  128.1 0.7 iota_compare_fusion.3
  128.8 0.3 fusion.25
  129.3 0.4 fusion.27
  129.7 0.6 dynamic_slice.40
  132.3 0.7 iota_compare_fusion.3
  133.4 0.4 fusion.27
  133.9 1.2 copy.51
  135.1 3.5 %all-to-all-start.3 = ((bf16[1,512,1,4,128]{4,3,2,0,1:T(4,128)(2,1)}), bf16[1,512,1,4,128]{4,3,2,0,1:T(4,128)(2,1)S(1)}, u32[]{:S(2)}, u32[]{:S(2)}) async-start(bf16[1,512,1,4,128]{4,3,2,0,1:T(4,128)(2,1)} %bitcast.54), calls=%async_computation.3 | async-start | bytes 1048576 | tf_op jit(solution)/shard_map/all_to_all | solution.py:99
  138.6 8.8 %all-to-all-done.3 = bf16[1,512,1,4,128]{4,3,2,0,1:T(4,128)(2,1)S(1)} async-done(((bf16[1,512,1,4,128]{4,3,2,0,1:T(4,128)(2,1)}), bf16[1,512,1,4,128]{4,3,2,0,1:T(4,128)(2,1)S(1)}, u32[]{:S(2)}, u32[]{:S(2)}) %all-to-all-start.3) | async-done | bytes 524320 | tf_op jit(solution)/shard_map/all_to_all | solution.py:99
  147.8 8.1 %gather_fusion = bf16[8,256,2048]{2,1,0:T(8,128)(2,1)} fusion(bf16[8,256,2048]{2,1,0:T(8,128)(2,1)} %all-gather.5.cloned.1.call-done, s32[1024]{0:T(1024)S(1)} %pad_clamp_fusion), kind=kCustom, calls=%fused_computation | custom fusion | bytes 16777248 | tf_op jit(solution)/shard_map/jit(_take)/gather | solution.py:103
  155.8 7.5 %broadcast_select_fusion = bf16[8,256,2048]{2,1,0:T(8,128)(2,1)} fusion(bf16[8,256,2048]{2,1,0:T(8,128)(2,1)} %gather_fusion, pred[8]{0:T(512)(128)(4,1)S(1)} %compare_and_fusion), kind=kLoop, calls=%fused_computation.18 | loop fusion | flops 4194304 | bytes 16777224 | tf_op jit(solution)/shard_map/jit(_take)/select_n | solution.py:103
  163.3 5.5 %fusion.12 = bf16[1,128,2048]{2,1,0:T(8,128)(2,1)} fusion(bf16[128,2048]{0,1:T(8,128)(2,1)S(1)} %bitcast.66, bf16[2048,2048]{1,0:T(8,128)(2,1)} %bitcast.65), kind=kOutput, calls=%fused_computation.20 | convolution fusion | flops 1074003968 | bytes 9437184 | tf_op jit(solution)/shard_map/dot_general | solution.py:104
  (31 shorter events, 3.0 us)
Async XLA Ops:
  7.2 61.4 %copy-start = (bf16[1,128,2048]{2,1,0:T(8,128)(2,1)S(1)}, bf16[1,128,2048]{2,1,0:T(8,128)(2,1)}, u32[]{:S(2)}) copy-start(bf16[1,128,2048]{2,1,0:T(8,128)(2,1)} %param.13) | copy-start | bytes 1572868
  7.2 77.0 %copy-start.1 = (bf16[1,128,2048]{2,1,0:T(8,128)(2,1)S(1)}, bf16[1,128,2048]{2,1,0:T(8,128)(2,1)}, u32[]{:S(2)}) copy-start(bf16[1,128,2048]{2,1,0:T(8,128)(2,1)} %param.11) | copy-start | bytes 1572868
  7.2 95.3 %copy-start.2 = (s32[8]{0:T(128)S(1)}, s32[8]{0:T(128)}, u32[]{:S(2)}) copy-start(s32[8]{0:T(128)} %param.19) | copy-start | bytes 100
  7.2 55.6 %all-gather.3.cloned.1.call-start = ((), (), s32[]{:S(2)}) async-start(), calls=%async_computation.4 | async-start | bytes 2359296 | tf_op jit(solution)/shard_map/all_gather | solution.py:101
  10.4 137.4 %all-gather.5.cloned.1.call-start = ((), (), s32[]{:S(2)}) async-start(), calls=%async_computation.5 | async-start | bytes 10485760 | tf_op jit(solution)/shard_map/all_gather | solution.py:102
  65.1 15.6 %all-to-all-start.1 = ((bf16[1,128,4,4,128]{4,1,3,0,2:T(8,128)(2,1)}), bf16[1,128,4,4,128]{4,1,3,0,2:T(8,128)(2,1)S(1)}, u32[]{:S(2)}, u32[]{:S(2)}) async-start(bf16[1,128,4,4,128]{4,1,3,0,2:T(8,128)(2,1)} %copy.42), calls=%async_computation.1 | async-start | bytes 1048576 | tf_op jit(solution)/shard_map/all_to_all | solution.py:83
  80.7 18.2 %all-to-all-start.2 = ((bf16[1,128,4,4,128]{4,1,3,0,2:T(8,128)(2,1)}), bf16[1,128,4,4,128]{4,1,3,0,2:T(8,128)(2,1)S(1)}, u32[]{:S(2)}, u32[]{:S(2)}) async-start(bf16[1,128,4,4,128]{4,1,3,0,2:T(8,128)(2,1)} %copy.45), calls=%async_computation.2 | async-start | bytes 1048576 | tf_op jit(solution)/shard_map/all_to_all | solution.py:86
  99.0 18.2 %all-to-all-start = ((bf16[1,128,4,4,128]{4,1,3,0,2:T(8,128)(2,1)}), bf16[1,128,4,4,128]{4,1,3,0,2:T(8,128)(2,1)S(1)}, u32[]{:S(2)}, u32[]{:S(2)}) async-start(bf16[1,128,4,4,128]{4,1,3,0,2:T(8,128)(2,1)} %copy.39), calls=%async_computation | async-start | bytes 1048576 | tf_op jit(solution)/shard_map/all_to_all | solution.py:80
  135.1 12.3 %all-to-all-start.3 = ((bf16[1,512,1,4,128]{4,3,2,0,1:T(4,128)(2,1)}), bf16[1,512,1,4,128]{4,3,2,0,1:T(4,128)(2,1)S(1)}, u32[]{:S(2)}, u32[]{:S(2)}) async-start(bf16[1,512,1,4,128]{4,3,2,0,1:T(4,128)(2,1)} %bitcast.54), calls=%async_computation.3 | async-start | bytes 1048576 | tf_op jit(solution)/shard_map/all_to_all | solution.py:99
Sparse Core Ops, SparseCore 0:
  10.7 51.9 all-gather.2
  64.3 71.0 all-gather.4
where the time goes:
time: 176 us
  waiting for transfers between devices  100 us (57%)
  local copies, waits for them, and re-layouts  17 us (10%)
  between operations  14.2 us (8%)
  other arithmetic  14.1 us (8%)
  starting transfers between devices  14 us (8%)
  matrix products  8.47 us (5%)
  loops' own time  7.88 us (4%)
    all_gather x1, waiting for transfers between devices, body(): owned = lax.all_gather(weight_half, 'dp', axis=0, tiled=True)  52.3 us
    all_to_all x1, waiting for transfers between devices, body(): lax.all_to_all(split_heads(queries), 'seq', split_axis=2, concat_axis=1,...  14.5 us
    all_to_all x1, waiting for transfers between devices, body(): lax.all_to_all(split_heads(hit_values), 'seq', split_axis=2, concat_axis=...  13.4 us
    all_to_all x1, waiting for transfers between devices, body(): lax.all_to_all(split_heads(hit_keys), 'seq', split_axis=2, concat_axis=1,...  10.8 us
    all_to_all x1, waiting for transfers between devices, body(): lax.all_to_all(attended, 'seq', split_axis=1, concat_axis=2, tiled=True)  8.77 us
    gather x1, local copies, waits for them, and re-layouts, body(): projection = jnp.take(full, inverse, axis=0).reshape(width, width)  8.08 us
    another operation x1, loops' own time, body(): outputs = lax.map(one_head, jnp.arange(n_heads, dtype=jnp.int32))  7.88 us
    select_n x2, other arithmetic, body(): projection = jnp.take(full, inverse, axis=0).reshape(width, width)  7.49 us
  transfers between devices with their start and end apart: 6, of which 5 were waited for; matrix products, arithmetic and copies ran while one was open for 9% of the time, Pallas kernels for 0%

commit v1 on v0

--- a/solution.py
+++ b/solution.py
@@ -11,6 +11,18 @@
 epsilon = 1e-08
 step_count = 10.0
 block_rows = 512
+
+
+def split_up(value, dim, size):
+    shape = value.shape
+    tiles = value.reshape(*shape[:dim], size, shape[dim] // size, *shape[dim + 1 :])
+    return jnp.moveaxis(tiles, dim, 0)
+
+
+def in_order(tiles, dim):
+    tiles = jnp.moveaxis(tiles, 0, dim)
+    dims = tiles.shape
+    return tiles.reshape(*dims[:dim], dims[dim] * dims[dim + 1], *dims[dim + 2 :])
 
 
 def adam_update(master_weight, first_moment, second_moment, gradient):
@@ -77,9 +89,15 @@
     def split_heads(array):
         return array.reshape(1, tok_rows, groups, heads_here, HEAD_DIM)
 
-    query_part = lax.all_to_all(
-        split_heads(queries), "seq", split_axis=2, concat_axis=1, tiled=True
-    )
+    value = split_heads(queries)
+    size, here = (lax.axis_size("seq"), lax.axis_index("seq"))
+    parts = split_up(value, 2, size)
+    outs = [parts[here]]
+    for hop in range(1, size):
+        sent = parts[here ^ hop]
+        outs.append(lax.ppermute(sent, "seq", [(i, i ^ hop) for i in range(size)]))
+    parts = jnp.stack(outs)[here ^ jnp.arange(size)]
+    query_part = in_order(parts, 1)
     keys_part = lax.all_to_all(
         split_heads(hit_keys), "seq", split_axis=2, concat_axis=1, tiled=True
     )

time: 176 us -> 169 us (0.960)
  waiting for transfers between devices: 100 us -> 95.3 us
    all_to_all x1 -> x0, waiting for transfers between devices: 14.5 us -> none  [body(): lax.all_to_all(split_heads(queries), 'seq', split_axis=2, concat_axis=1,...]
    ppermute x0 -> x3, waiting for transfers between devices: none -> 7.6 us  [body(): outs.append(lax.ppermute(sent, 'seq', [(i, i ^ hop) for i in range(size)]))]
    all_to_all x1, waiting for transfers between devices: 8.77 us -> 14.7 us  [body(): lax.all_to_all(attended, 'seq', split_axis=1, concat_axis=2, tiled=True)]
    all_to_all x1, waiting for transfers between devices: 13.4 us -> 9.94 us  [body(): lax.all_to_all(split_heads(hit_values), 'seq', split_axis=2, concat_axis=...]
    all_to_all x1 -> x0, starting transfers between devices: 3.47 us -> none  [body(): lax.all_to_all(split_heads(queries), 'seq', split_axis=2, concat_axis=1,...]
    all_to_all x1, waiting for transfers between devices: 10.8 us -> 8.29 us  [body(): lax.all_to_all(split_heads(hit_keys), 'seq', split_axis=2, concat_axis=1,...]
    all_gather x1, waiting for transfers between devices: 0.02 us -> 2.36 us  [body(): full = lax.all_gather(owned, 'seq', axis=2, tiled=True)]
    ppermute x0 -> x3, starting transfers between devices: none -> 2.34 us  [body(): outs.append(lax.ppermute(sent, 'seq', [(i, i ^ hop) for i in range(size)]))]
  transfers between devices with their start and end apart: 6 -> 8, of which waited for: 5 -> 7; matrix products, arithmetic and copies ran while one was open for 9% -> 9% of each run, Pallas kernels for 0% -> 0%
where the time goes in v1:
time: 169 us
  waiting for transfers between devices  95.3 us (56%)
  local copies, waits for them, and re-layouts  17 us (10%)
  between operations  14.3 us (8%)
  other arithmetic  14.2 us (8%)
  starting transfers between devices  12.8 us (8%)
  matrix products  8.46 us (5%)
  loops' own time  6.83 us (4%)
    all_gather x1, waiting for transfers between devices, body(): owned = lax.all_gather(weight_half, 'dp', axis=0, tiled=True)  52.3 us
    all_to_all x1, waiting for transfers between devices, body(): lax.all_to_all(attended, 'seq', split_axis=1, concat_axis=2, tiled=True)  14.7 us
    all_to_all x1, waiting for transfers between devices, body(): lax.all_to_all(split_heads(hit_values), 'seq', split_axis=2, concat_axis=...  9.94 us
    all_to_all x1, waiting for transfers between devices, body(): lax.all_to_all(split_heads(hit_keys), 'seq', split_axis=2, concat_axis=1,...  8.29 us
    gather x1, local copies, waits for them, and re-layouts, body(): projection = jnp.take(full, inverse, axis=0).reshape(width, width)  8.06 us
    ppermute x3, waiting for transfers between devices, body(): outs.append(lax.ppermute(sent, 'seq', [(i, i ^ hop) for i in range(size)]))  7.6 us
    select_n x2, other arithmetic, body(): projection = jnp.take(full, inverse, axis=0).reshape(width, width)  7.48 us
    another operation x1, loops' own time, body(): outputs = lax.map(one_head, jnp.arange(n_heads, dtype=jnp.int32))  6.83 us
  transfers between devices with their start and end apart: 8, of which 7 were waited for; matrix products, arithmetic and copies ran while one was open for 9% of the time, Pallas kernels for 0%

profile of v1, /device:TPU:0, one launch (start us, length us, event | category | flops | bytes accessed | tf_op | source)
XLA Modules:
  0.0 168.8 jit_solution(13523199143963764991)
XLA Ops:
  7.2 3.1 %fusion.16 = (bf16[1,256,512]{2,1,0:T(8,128)(2,1)}, f32[1,256,512]{2,1,0:T(8,128)}, f32[1,256,512]{2,1,0:T(8,128)}, f32[1,256,512]{2,1,0:T(8,128)}) fusion(f32[1,256,512]{2,1,0:T(8,128)} %param.15, f32[1,256,512]{2,1,0:T(8,128)} %param.18, f32[1,256,512]{2,1,0:T(8,128)} %param.16, f32[1,256,512]{2,1,0:T(8,128)} %param.17), kind=kLoop, calls=%fused_computation.46 | loop fusion | flops 2097152 | bytes 3932160 | tf_op jit(solution)/shard_map/convert_element_type | solution.py:78
  10.4 52.3 %all-gather.3.cloned.1.call-done = bf16[8,256,512]{2,1,0:T(8,128)(2,1)} async-done(((bf16[1,256,512]{2,1,0:T(8,128)(2,1)}), bf16[8,256,512]{2,1,0:T(8,128)(2,1)}) %all-gather.3.cloned.1.call-update) | async-done | bytes 2097168 | tf_op jit(solution)/shard_map/all_gather | solution.py:119
  62.8 1.3 copy.59
  64.1 1.0 copy.60
  65.1 3.5 %all-to-all-start = ((bf16[1,128,4,4,128]{4,1,3,0,2:T(8,128)(2,1)}), bf16[1,128,4,4,128]{4,1,3,0,2:T(8,128)(2,1)S(1)}, u32[]{:S(2)}, u32[]{:S(2)}) async-start(bf16[1,128,4,4,128]{4,1,3,0,2:T(8,128)(2,1)} %copy.60), calls=%async_computation | async-start | bytes 1048576 | tf_op jit(solution)/shard_map/all_to_all | solution.py:101
  69.2 1.8 %collective-permute-start.2 = (bf16[1,128,1,4,128]{4,1,3,2,0:T(8,128)(2,1)S(1)}, bf16[1,128,1,4,128]{4,1,3,2,0:T(8,128)(2,1)S(1)}, u32[]{:S(2)}, u32[]{:S(2)}) collective-permute-start(bf16[1,128,1,4,128]{4,1,3,2,0:T(8,128)(2,1)S(1)} %bitcast.88), channel_id=1, source_target_pairs={{0,3},{1,2},{2,1},{3,0},{4,7},{5,6},{6,5},{7,4},{8,11},{9,10},{10,... | collective-permute-start | bytes 393224 | tf_op jit(solution)/shard_map/ppermute | solution.py:98
  71.9 1.0 copy.63
  72.9 8.3 %all-to-all-done = bf16[1,128,4,4,128]{4,1,3,0,2:T(8,128)(2,1)S(1)} async-done(((bf16[1,128,4,4,128]{4,1,3,0,2:T(8,128)(2,1)}), bf16[1,128,4,4,128]{4,1,3,0,2:T(8,128)(2,1)S(1)}, u32[]{:S(2)}, u32[]{:S(2)}) %all-to-all-start) | async-done | bytes 524320 | tf_op jit(solution)/shard_map/all_to_all | solution.py:101
  81.2 3.5 %all-to-all-start.1 = ((bf16[1,128,4,4,128]{4,1,3,0,2:T(8,128)(2,1)}), bf16[1,128,4,4,128]{4,1,3,0,2:T(8,128)(2,1)S(1)}, u32[]{:S(2)}, u32[]{:S(2)}) async-start(bf16[1,128,4,4,128]{4,1,3,0,2:T(8,128)(2,1)} %copy.63), calls=%async_computation.1 | async-start | bytes 1048576 | tf_op jit(solution)/shard_map/all_to_all | solution.py:104
  84.9 7.5 %collective-permute-done.1 = bf16[1,128,1,4,128]{4,1,3,2,0:T(8,128)(2,1)S(1)} collective-permute-done((bf16[1,128,1,4,128]{4,1,3,2,0:T(8,128)(2,1)S(1)}, bf16[1,128,1,4,128]{4,1,3,2,0:T(8,128)(2,1)S(1)}, u32[]{:S(2)}, u32[]{:S(2)}) %collective-permute-start.1) | collective-permute-done | bytes 131104 | tf_op jit(solution)/shard_map/ppermute | solution.py:98
  92.5 0.6 gather_fusion
  93.3 9.9 %all-to-all-done.1 = bf16[1,128,4,4,128]{4,1,3,0,2:T(8,128)(2,1)S(1)} async-done(((bf16[1,128,4,4,128]{4,1,3,0,2:T(8,128)(2,1)}), bf16[1,128,4,4,128]{4,1,3,0,2:T(8,128)(2,1)S(1)}, u32[]{:S(2)}, u32[]{:S(2)}) %all-to-all-start.1) | async-done | bytes 524320 | tf_op jit(solution)/shard_map/all_to_all | solution.py:104
  103.3 15.6 %while.10 = (s32[]{:T(128)}, bf16[4,512,128]{2,1,0:T(8,128)(2,1)S(1)}, s32[]{:T(128)}, s32[4]{0:T(128)S(1)}, bf16[1,512,1,4,128]{4,1,3,2,0:T(8,128)(2,1)S(1)}, /...) while((s32[]{:T(128)}, ...), condition=%wide.region_3.4_spmd, body=%wide.region_0.3_spmd.sunk | while | flops 136379904 | bytes 3682471 | solution.py:115
  103.3 0.6 dynamic_slice.47
  105.5 0.7 iota_compare_fusion.3
  106.7 0.4 fusion.28
  107.2 0.6 dynamic_slice.47
  109.4 0.7 iota_compare_fusion.3
  110.6 0.4 fusion.28
  111.0 0.6 dynamic_slice.47
  113.3 0.7 iota_compare_fusion.3
  114.5 0.4 fusion.28
  114.9 0.6 dynamic_slice.47
  117.2 0.7 iota_compare_fusion.3
  118.4 0.4 fusion.28
  118.8 1.2 copy.77
  120.0 3.5 %all-to-all-start.2 = ((bf16[1,512,1,4,128]{4,3,2,0,1:T(4,128)(2,1)}), bf16[1,512,1,4,128]{4,3,2,0,1:T(4,128)(2,1)S(1)}, u32[]{:S(2)}, u32[]{:S(2)}) async-start(bf16[1,512,1,4,128]{4,3,2,0,1:T(4,128)(2,1)} %bitcast.64), calls=%async_computation.2 | async-start | bytes 1048576 | tf_op jit(solution)/shard_map/all_to_all | solution.py:117
  123.5 14.7 %all-to-all-done.2 = bf16[1,512,1,4,128]{4,3,2,0,1:T(4,128)(2,1)S(1)} async-done(((bf16[1,512,1,4,128]{4,3,2,0,1:T(4,128)(2,1)}), bf16[1,512,1,4,128]{4,3,2,0,1:T(4,128)(2,1)S(1)}, u32[]{:S(2)}, u32[]{:S(2)}) %all-to-all-start.2) | async-done | bytes 524320 | tf_op jit(solution)/shard_map/all_to_all | solution.py:117
  138.6 2.4 %all-gather.5.cloned.1.call-done = bf16[8,256,2048]{2,1,0:T(8,128)(2,1)} async-done(((bf16[8,256,512]{2,1,0:T(8,128)(2,1)}), bf16[8,256,2048]{2,1,0:T(8,128)(2,1)}) %all-gather.5.cloned.1.call-update) | async-done | bytes 8388624 | tf_op jit(solution)/shard_map/all_gather | solution.py:120
  141.0 8.1 %gather_fusion.1 = bf16[8,256,2048]{2,1,0:T(8,128)(2,1)} fusion(bf16[8,256,2048]{2,1,0:T(8,128)(2,1)} %all-gather.5.cloned.1.call-done, s32[1024]{0:T(1024)S(1)} %pad_clamp_fusion), kind=kCustom, calls=%fused_computation.1 | custom fusion | bytes 16777248 | tf_op jit(solution)/shard_map/jit(_take)/gather | solution.py:121
  149.0 7.5 %broadcast_select_fusion = bf16[8,256,2048]{2,1,0:T(8,128)(2,1)} fusion(bf16[8,256,2048]{2,1,0:T(8,128)(2,1)} %gather_fusion.1, pred[8]{0:T(512)(128)(4,1)S(1)} %compare_and_fusion), kind=kLoop, calls=%fused_computation.19 | loop fusion | flops 4194304 | bytes 16777224 | tf_op jit(solution)/shard_map/jit(_take)/select_n | solution.py:121
  156.5 5.5 %fusion.12 = bf16[1,128,2048]{2,1,0:T(8,128)(2,1)} fusion(bf16[128,2048]{0,1:T(8,128)(2,1)S(1)} %bitcast.80, bf16[2048,2048]{1,0:T(8,128)(2,1)} %bitcast.79), kind=kOutput, calls=%fused_computation.21 | convolution fusion | flops 1074003968 | bytes 9437184 | tf_op jit(solution)/shard_map/dot_general | solution.py:122
  (43 shorter events, 4.4 us)
Async XLA Ops:
  7.2 61.4 %copy-start = (bf16[1,128,2048]{2,1,0:T(8,128)(2,1)S(1)}, bf16[1,128,2048]{2,1,0:T(8,128)(2,1)}, u32[]{:S(2)}) copy-start(bf16[1,128,2048]{2,1,0:T(8,128)(2,1)} %param.11) | copy-start | bytes 1572868
  7.2 64.4 %copy-start.1 = (bf16[1,128,2048]{2,1,0:T(8,128)(2,1)S(1)}, bf16[1,128,2048]{2,1,0:T(8,128)(2,1)}, u32[]{:S(2)}) copy-start(bf16[1,128,2048]{2,1,0:T(8,128)(2,1)} %param.13) | copy-start | bytes 1572868
  7.2 77.6 %copy-start.2 = (s32[8]{0:T(128)S(1)}, s32[8]{0:T(128)}, u32[]{:S(2)}) copy-start(s32[8]{0:T(128)} %param.19) | copy-start | bytes 100
  7.2 55.6 %all-gather.3.cloned.1.call-start = ((), (), s32[]{:S(2)}) async-start(), calls=%async_computation.3 | async-start | bytes 2359296 | tf_op jit(solution)/shard_map/all_gather | solution.py:119
  10.4 130.6 %all-gather.5.cloned.1.call-start = ((), (), s32[]{:S(2)}) async-start(), calls=%async_computation.4 | async-start | bytes 10485760 | tf_op jit(solution)/shard_map/all_gather | solution.py:120
  65.1 16.1 %all-to-all-start = ((bf16[1,128,4,4,128]{4,1,3,0,2:T(8,128)(2,1)}), bf16[1,128,4,4,128]{4,1,3,0,2:T(8,128)(2,1)S(1)}, u32[]{:S(2)}, u32[]{:S(2)}) async-start(bf16[1,128,4,4,128]{4,1,3,0,2:T(8,128)(2,1)} %copy.60), calls=%async_computation | async-start | bytes 1048576 | tf_op jit(solution)/shard_map/all_to_all | solution.py:101
  69.2 15.7 %collective-permute-start.2 = (bf16[1,128,1,4,128]{4,1,3,2,0:T(8,128)(2,1)S(1)}, bf16[1,128,1,4,128]{4,1,3,2,0:T(8,128)(2,1)S(1)}, u32[]{:S(2)}, u32[]{:S(2)}) collective-permute-start(bf16[1,128,1,4,128]{4,1,3,2,0:T(8,128)(2,1)S(1)} %bitcast.88), channel_id=1, source_target_pairs={{0,3},{1,2},{2,1},{3,0},{4,7},{5,6},{6,5},{7,4},{8,11},{9,10},{10,... | collective-permute-start | bytes 393224 | tf_op jit(solution)/shard_map/ppermute | solution.py:98
  71.0 13.9 %collective-permute-start = (bf16[1,128,1,4,128]{4,1,3,2,0:T(8,128)(2,1)S(1)}, bf16[1,128,1,4,128]{4,1,3,2,0:T(8,128)(2,1)S(1)}, u32[]{:S(2)}, u32[]{:S(2)}) collective-permute-start(bf16[1,128,1,4,128]{4,1,3,2,0:T(8,128)(2,1)S(1)} %bitcast.89), channel_id=1, source_target_pairs={{0,1},{1,0},{2,3},{3,2},{4,5},{5,4},{6,7},{7,6},{8,9},{9,8},{10,11... | collective-permute-start | bytes 393224 | tf_op jit(solution)/shard_map/ppermute | solution.py:98
  71.5 21.0 %collective-permute-start.1 = (bf16[1,128,1,4,128]{4,1,3,2,0:T(8,128)(2,1)S(1)}, bf16[1,128,1,4,128]{4,1,3,2,0:T(8,128)(2,1)S(1)}, u32[]{:S(2)}, u32[]{:S(2)}) collective-permute-start(bf16[1,128,1,4,128]{4,1,3,2,0:T(8,128)(2,1)S(1)} %bitcast.90), channel_id=1, source_target_pairs={{0,2},{1,3},{2,0},{3,1},{4,6},{5,7},{6,4},{7,5},{8,10},{9,11},{10,... | collective-permute-start | bytes 393224 | tf_op jit(solution)/shard_map/ppermute | solution.py:98
  81.2 22.0 %all-to-all-start.1 = ((bf16[1,128,4,4,128]{4,1,3,0,2:T(8,128)(2,1)}), bf16[1,128,4,4,128]{4,1,3,0,2:T(8,128)(2,1)S(1)}, u32[]{:S(2)}, u32[]{:S(2)}) async-start(bf16[1,128,4,4,128]{4,1,3,0,2:T(8,128)(2,1)} %copy.63), calls=%async_computation.1 | async-start | bytes 1048576 | tf_op jit(solution)/shard_map/all_to_all | solution.py:104
  120.0 18.2 %all-to-all-start.2 = ((bf16[1,512,1,4,128]{4,3,2,0,1:T(4,128)(2,1)}), bf16[1,512,1,4,128]{4,3,2,0,1:T(4,128)(2,1)S(1)}, u32[]{:S(2)}, u32[]{:S(2)}) async-start(bf16[1,512,1,4,128]{4,3,2,0,1:T(4,128)(2,1)} %bitcast.64), calls=%async_computation.2 | async-start | bytes 1048576 | tf_op jit(solution)/shard_map/all_to_all | solution.py:117
Sparse Core Ops, SparseCore 0:
  10.7 51.9 all-gather.2
  64.3 76.6 all-gather.4
